TPU v7x, 32 devices: a whole 2x2x4 slice. The times are simulated.
32 devices in a mesh: fsdp: 8 (over y, x, core), tp: 4 (over z).
Axes of the slice: x: 2, y: 2, z: 4, core: 2. Of those that a mesh axis runs over, the one named last changes fastest.
Arguments:
- layer_input: bfloat16 [24576, 512], P(('fsdp', 'tp')), may hold values from -6 to 6
- segment_ids: int32 [24, 1024], P('fsdp'), may hold values from 0 to 15, never falling along the last dimension, each value on 1 to 512 neighbouring positions
- valid_mask: int32 [24576], P(('fsdp', 'tp')), may hold values from 0 to 1, as said below
- teacher: bfloat16 [24576, 512], P(('fsdp', 'tp')), may hold values from -6 to 6
- cotangent: bfloat16 [24576, 512], P(('fsdp', 'tp')), may hold values from -6 to 6
- ln1_gain: bfloat16 [512], P('fsdp'), may hold values from 0.099609375 to 1.8984375
- ln1_bias: bfloat16 [512], P('fsdp'), may hold values from -1.75 to 1.75
- w_q: bfloat16 [512, 512], P('fsdp', 'tp'), may hold values from -0.25 to 0.25
- w_k: bfloat16 [512, 512], P('fsdp', 'tp'), may hold values from -0.25 to 0.25
- w_v: bfloat16 [512, 512], P('fsdp', 'tp'), may hold values from -0.25 to 0.25
- b_q: bfloat16 [8, 64], P('tp', 'fsdp'), may hold values from -3 to 3
- b_v: bfloat16 [8, 64], P('tp', 'fsdp'), may hold values from -3 to 3
- w_o: bfloat16 [512, 512], P('tp', 'fsdp'), may hold values from -1 to 1
- b_o: bfloat16 [512], P('fsdp'), may hold values from -3 to 3
- ln2_gain: bfloat16 [512], P('fsdp'), may hold values from 0.099609375 to 1.8984375
- ln2_bias: bfloat16 [512], P('fsdp'), may hold values from -1.75 to 1.75
- w_up: bfloat16 [512, 2048], P('fsdp', 'tp'), may hold values from -0.25 to 0.25
- b_up: bfloat16 [32, 64], P('tp', 'fsdp'), may hold values from -3 to 3
- w_down: bfloat16 [2048, 512], P('tp', 'fsdp'), may hold values from -0.25 to 0.25
- b_down: bfloat16 [512], P('fsdp'), may hold values from -3 to 3
Outputs:
- layer_out: bfloat16 [24576, 512], P(('fsdp', 'tp'))
- loss: float32 [], replicated
- grad_layer_input: float32 [24576, 512], P(('fsdp', 'tp'))
- grad_ln1_gain: float32 [512], P('fsdp')
- grad_ln1_bias: float32 [512], P('fsdp')
- grad_w_q: float32 [512, 512], P('fsdp', 'tp')
- grad_w_k: float32 [512, 512], P('fsdp', 'tp')
- grad_w_v: float32 [512, 512], P('fsdp', 'tp')
- grad_b_q: float32 [8, 64], P('tp', 'fsdp')
- grad_b_v: float32 [8, 64], P('tp', 'fsdp')
- grad_w_o: float32 [512, 512], P('tp', 'fsdp')
- grad_b_o: float32 [512], P('fsdp')
- grad_ln2_gain: float32 [512], P('fsdp')
- grad_ln2_bias: float32 [512], P('fsdp')
- grad_w_up: float32 [512, 2048], P('fsdp', 'tp')
- grad_b_up: float32 [32, 64], P('tp', 'fsdp')
- grad_w_down: float32 [2048, 512], P('tp', 'fsdp')
- grad_b_down: float32 [512], P('fsdp')
Inputs may be any that keep to these rules, and one draw needn't show every extreme that they name: `segment_ids`: in each sequence the ids never fall, each document holds 1 to 512 positions, and one holds exactly 512. `valid_mask`: the first token of every sequence is 1.
All inputs are finite; a program needn't handle non-finite values.
Results may differ from a plain program's by a relative error of at most 0.014.
Values may be sent and summed in bfloat16 or wider, within the bound.
No kernel may reach another device: no remote copies, remote signals or barrier semaphores. Data moves between devices by JAX's collectives and lax.ppermute only.
A program may use at most 128 MiB of HBM per device.

v0:
```python
import jax
import jax.numpy as jnp
from jax import lax
from jax.sharding import PartitionSpec as P

D = 512
HD = 64
LEN = 1024


def layer_norm(values, gains, offsets):
    center = values - jnp.mean(values, axis=-1, keepdims=True)
    spread = jnp.mean(center * center, axis=-1, keepdims=True)
    return center * lax.rsqrt(spread + 1e-05) * gains + offsets


def quick_gelu(values):
    return values * jax.nn.sigmoid(1.702 * values)


def block_scores(query_block, key_seq, segment_seq, first_row):
    block_rows = query_block.shape[0]
    query_place = first_row + jnp.arange(block_rows, dtype=jnp.int32)
    key_place = jnp.arange(key_seq.shape[0], dtype=jnp.int32)
    query_segment = lax.dynamic_slice_in_dim(segment_seq, first_row, block_rows)
    allowed = (query_segment[:, None] == segment_seq[None, :]) & (
        key_place[None, :] <= query_place[:, None]
    )
    raw_scores = jnp.einsum(
        "qhd,khd->hqk", query_block, key_seq, preferred_element_type=jnp.float32
    ) * HD ** (-0.5)
    return jnp.where(allowed[None], raw_scores, -1e30)


def forward_sequence(inputs):
    query_seq, key_seq, value_seq, segment_seq = inputs

    def forward_one_block(element):
        block_index, query_block = element
        scores = block_scores(query_block, key_seq, segment_seq, block_index * query_block.shape[0])
        row_max = jnp.max(scores, axis=-1, keepdims=True)
        exponent = jnp.exp(scores - row_max)
        row_sum = jnp.sum(exponent, axis=-1, keepdims=True)
        weights = (exponent / row_sum).astype(jnp.bfloat16)
        attended = jnp.einsum(
            "hqk,khd->qhd", weights, value_seq, preferred_element_type=jnp.float32
        )
        return (attended.astype(jnp.bfloat16), (row_max + jnp.log(row_sum))[..., 0])

    return lax.map(forward_one_block, (jnp.arange(query_seq.shape[0], dtype=jnp.int32), query_seq))


def backward_sequence(inputs):
    query_seq, key_seq, value_seq, segment_seq, total_seq, grad_out_seq = inputs
    zero_grads = jnp.zeros(key_seq.shape, jnp.float32)

    def backward_one_block(carried, element):
        grad_keys, grad_values = carried
        block_index, query_block, total_block, grad_block = element
        scores = block_scores(query_block, key_seq, segment_seq, block_index * query_block.shape[0])
        weights = jnp.exp(scores - total_block[..., None])
        grad_values = grad_values + jnp.einsum(
            "hqk,qhd->khd",
            weights.astype(jnp.bfloat16),
            grad_block,
            preferred_element_type=jnp.float32,
        )
        grad_weights = jnp.einsum(
            "qhd,khd->hqk", grad_block, value_seq, preferred_element_type=jnp.float32
        )
        grad_scores = (
            weights * (grad_weights - jnp.sum(weights * grad_weights, axis=-1, keepdims=True))
        ).astype(jnp.bfloat16)
        grad_query = jnp.einsum(
            "hqk,khd->qhd", grad_scores, key_seq, preferred_element_type=jnp.float32
        ) * HD ** (-0.5)
        grad_keys = grad_keys + jnp.einsum(
            "hqk,qhd->khd", grad_scores, query_block, preferred_element_type=jnp.float32
        ) * HD ** (-0.5)
        return ((grad_keys, grad_values), grad_query.astype(jnp.bfloat16))

    (grad_keys, grad_values), grad_queries = lax.scan(
        backward_one_block,
        (zero_grads, zero_grads),
        (jnp.arange(query_seq.shape[0], dtype=jnp.int32), query_seq, total_seq, grad_out_seq),
    )
    return (grad_queries, grad_keys.astype(jnp.bfloat16), grad_values.astype(jnp.bfloat16))


def local(
    layer_input,
    segment_ids,
    valid_mask,
    teacher,
    cotangent,
    ln1_gain,
    ln1_bias,
    w_q,
    w_k,
    w_v,
    b_q,
    b_v,
    w_o,
    b_o,
    ln2_gain,
    ln2_bias,
    w_up,
    b_up,
    w_down,
    b_down,
):
    fsdp_size = lax.axis_size("fsdp")
    tensor_size = lax.axis_size("tp")
    local_rows = layer_input.shape[0]
    (
        gain_one,
        bias_one,
        query_w,
        key_w,
        value_w,
        query_b,
        value_b,
        out_w,
        out_b,
        gain_two,
        bias_two,
        upper_w,
        upper_b,
        lower_w,
        lower_b,
    ) = (
        lax.all_gather(ln1_gain, "fsdp", axis=0, tiled=True),
        lax.all_gather(ln1_bias, "fsdp", axis=0, tiled=True),
        lax.all_gather(w_q, "fsdp", axis=0, tiled=True),
        lax.all_gather(w_k, "fsdp", axis=0, tiled=True),
        lax.all_gather(w_v, "fsdp", axis=0, tiled=True),
        lax.all_gather(b_q, "fsdp", axis=1, tiled=True),
        lax.all_gather(b_v, "fsdp", axis=1, tiled=True),
        lax.all_gather(w_o, "fsdp", axis=1, tiled=True),
        lax.all_gather(b_o, "fsdp", axis=0, tiled=True),
        lax.all_gather(ln2_gain, "fsdp", axis=0, tiled=True),
        lax.all_gather(ln2_bias, "fsdp", axis=0, tiled=True),
        lax.all_gather(w_up, "fsdp", axis=0, tiled=True),
        lax.all_gather(b_up, "fsdp", axis=1, tiled=True),
        lax.all_gather(w_down, "fsdp", axis=1, tiled=True),
        lax.all_gather(b_down, "fsdp", axis=0, tiled=True),
    )
    mask_float = valid_mask.astype(jnp.float32)
    valid_total = lax.psum(jnp.sum(mask_float), ("fsdp", "tp"))
    tokens_all = local_rows * fsdp_size * tensor_size
    input_float = layer_input.astype(jnp.float32)
    gain_first = gain_one.astype(jnp.float32)
    bias_first = bias_one.astype(jnp.float32)
    gain_second = gain_two.astype(jnp.float32)
    bias_second = bias_two.astype(jnp.float32)
    normed_one = layer_norm(input_float, gain_first, bias_first).astype(jnp.bfloat16)
    head_count = query_w.shape[1] // HD
    rows_one = lax.all_gather(normed_one, "tp", axis=0, tiled=True)
    queries = (
        jnp.dot(rows_one, query_w, preferred_element_type=jnp.float32)
        + query_b.reshape(-1).astype(jnp.float32)
    ).astype(jnp.bfloat16)
    keys_all = jnp.dot(rows_one, key_w, preferred_element_type=jnp.float32).astype(jnp.bfloat16)
    values_all = (
        jnp.dot(rows_one, value_w, preferred_element_type=jnp.float32)
        + value_b.reshape(-1).astype(jnp.float32)
    ).astype(jnp.bfloat16)
    seq_count = segment_ids.shape[0]
    block_rows = min(512, LEN)
    block_count = LEN // block_rows
    shaped_queries = queries.reshape(seq_count, block_count, block_rows, head_count, HD)
    shaped_keys = keys_all.reshape(seq_count, LEN, head_count, HD)
    shaped_values = values_all.reshape(seq_count, LEN, head_count, HD)
    attended, log_totals = lax.map(
        forward_sequence, (shaped_queries, shaped_keys, shaped_values, segment_ids)
    )
    attended = attended.reshape(-1, head_count * HD)
    attention = lax.psum_scatter(
        jnp.dot(attended, out_w, preferred_element_type=jnp.float32).astype(jnp.bfloat16),
        "tp",
        scatter_dimension=0,
        tiled=True,
    ).astype(jnp.float32)
    hidden_one = input_float + attention + out_b.astype(jnp.float32)
    normed_two = layer_norm(hidden_one, gain_second, bias_second).astype(jnp.bfloat16)
    rows_two = lax.all_gather(normed_two, "tp", axis=0, tiled=True)
    pre_act = jnp.dot(rows_two, upper_w, preferred_element_type=jnp.float32) + upper_b.reshape(
        -1
    ).astype(jnp.float32)
    activated = quick_gelu(pre_act).astype(jnp.bfloat16)
    branch = lax.psum_scatter(
        jnp.dot(activated, lower_w, preferred_element_type=jnp.float32).astype(jnp.bfloat16),
        "tp",
        scatter_dimension=0,
        tiled=True,
    ).astype(jnp.float32)
    out_full = hidden_one + branch + lower_b.astype(jnp.float32)
    difference = out_full - teacher.astype(jnp.float32)
    square_part = jnp.sum(mask_float * jnp.mean(difference * difference, axis=-1))
    grad_out = (
        cotangent.astype(jnp.float32) + tokens_all / valid_total * mask_float[:, None] * difference
    )
    grad_lower_bias = jnp.sum(grad_out, axis=0)
    grad_out_low = grad_out.astype(jnp.bfloat16)
    grad_rows = lax.all_gather(grad_out_low, "tp", axis=0, tiled=True)
    grad_hidden_units = jnp.einsum(
        "nd,fd->nf", grad_rows, lower_w, preferred_element_type=jnp.float32
    )
    grad_lower = jnp.einsum("nf,nd->fd", activated, grad_rows, preferred_element_type=jnp.float32)
    gelu_value, gelu_pull = jax.vjp(quick_gelu, pre_act)
    grad_pre = gelu_pull(grad_hidden_units)[0].astype(jnp.bfloat16)
    grad_upper = jnp.einsum("nd,nf->df", rows_two, grad_pre, preferred_element_type=jnp.float32)
    grad_upper_bias = jnp.sum(grad_pre, axis=0, dtype=jnp.float32).reshape(upper_b.shape)
    grad_normed_two = lax.psum_scatter(
        jnp.einsum("nf,df->nd", grad_pre, upper_w, preferred_element_type=jnp.float32).astype(
            jnp.bfloat16
        ),
        "tp",
        scatter_dimension=0,
        tiled=True,
    ).astype(jnp.float32)
    norm_value, second_pull = jax.vjp(layer_norm, hidden_one, gain_second, bias_second)
    grad_hidden_norm, grad_gain_second, grad_bias_second = second_pull(grad_normed_two)
    grad_hidden = grad_out + grad_hidden_norm
    grad_out_bias = jnp.sum(grad_hidden, axis=0)
    grad_attn_low = grad_hidden.astype(jnp.bfloat16)
    grad_attn_rows = lax.all_gather(grad_attn_low, "tp", axis=0, tiled=True)
    grad_out_w = jnp.einsum(
        "nc,nd->cd", attended, grad_attn_rows, preferred_element_type=jnp.float32
    )
    grad_attended = jnp.einsum(
        "nd,cd->nc", grad_attn_rows, out_w, preferred_element_type=jnp.float32
    ).astype(jnp.bfloat16)
    grad_queries, grad_keys, grad_values = lax.map(
        backward_sequence,
        (
            shaped_queries,
            shaped_keys,
            shaped_values,
            segment_ids,
            log_totals,
            grad_attended.reshape(seq_count, block_count, block_rows, head_count, HD),
        ),
    )
    flat_queries = grad_queries.reshape(-1, head_count * HD)
    flat_keys = grad_keys.reshape(-1, head_count * HD)
    flat_values = grad_values.reshape(-1, head_count * HD)
    grad_query_w = jnp.einsum(
        "nd,nc->dc", rows_one, flat_queries, preferred_element_type=jnp.float32
    )
    grad_key_w = jnp.einsum("nd,nc->dc", rows_one, flat_keys, preferred_element_type=jnp.float32)
    grad_value_w = jnp.einsum(
        "nd,nc->dc", rows_one, flat_values, preferred_element_type=jnp.float32
    )
    grad_query_b = jnp.sum(flat_queries, axis=0, dtype=jnp.float32).reshape(query_b.shape)
    grad_value_b = jnp.sum(flat_values, axis=0, dtype=jnp.float32).reshape(value_b.shape)
    stacked_grads = jnp.concatenate((flat_queries, flat_keys, flat_values), axis=1)
    stacked_weights = jnp.concatenate((query_w, key_w, value_w), axis=1)
    grad_normed_one = lax.psum_scatter(
        jnp.einsum(
            "nc,dc->nd", stacked_grads, stacked_weights, preferred_element_type=jnp.float32
        ).astype(jnp.bfloat16),
        "tp",
        scatter_dimension=0,
        tiled=True,
    ).astype(jnp.float32)
    first_value, first_pull = jax.vjp(layer_norm, input_float, gain_first, bias_first)
    grad_input_norm, grad_gain_first, grad_bias_first = first_pull(grad_normed_one)
    grad_input = grad_hidden + grad_input_norm
    summed = lax.psum(
        (
            square_part,
            grad_gain_first,
            grad_bias_first,
            grad_out_bias,
            grad_gain_second,
            grad_bias_second,
            grad_lower_bias,
        ),
        ("fsdp", "tp"),
    )
    piece_size = D // fsdp_size
    piece_start = lax.axis_index("fsdp") * piece_size

    def own_piece(vector):
        return lax.dynamic_slice_in_dim(vector, piece_start, piece_size)

    loss = 0.5 * summed[0] / valid_total
    grad_wq, grad_wk, grad_wv, grad_bq, grad_bv, grad_wo, grad_wu, grad_bu, grad_wd = (
        lax.psum_scatter(
            grad_query_w.astype(jnp.bfloat16), "fsdp", scatter_dimension=0, tiled=True
        ).astype(jnp.float32),
        lax.psum_scatter(
            grad_key_w.astype(jnp.bfloat16), "fsdp", scatter_dimension=0, tiled=True
        ).astype(jnp.float32),
        lax.psum_scatter(
            grad_value_w.astype(jnp.bfloat16), "fsdp", scatter_dimension=0, tiled=True
        ).astype(jnp.float32),
        lax.psum_scatter(
            grad_query_b.astype(jnp.bfloat16), "fsdp", scatter_dimension=1, tiled=True
        ).astype(jnp.float32),
        lax.psum_scatter(
            grad_value_b.astype(jnp.bfloat16), "fsdp", scatter_dimension=1, tiled=True
        ).astype(jnp.float32),
        lax.psum_scatter(
            grad_out_w.astype(jnp.bfloat16), "fsdp", scatter_dimension=1, tiled=True
        ).astype(jnp.float32),
        lax.psum_scatter(
            grad_upper.astype(jnp.bfloat16), "fsdp", scatter_dimension=0, tiled=True
        ).astype(jnp.float32),
        lax.psum_scatter(
            grad_upper_bias.astype(jnp.bfloat16), "fsdp", scatter_dimension=1, tiled=True
        ).astype(jnp.float32),
        lax.psum_scatter(
            grad_lower.astype(jnp.bfloat16), "fsdp", scatter_dimension=1, tiled=True
        ).astype(jnp.float32),
    )
    return (
        out_full.astype(jnp.bfloat16),
        loss,
        grad_input,
        own_piece(summed[1]),
        own_piece(summed[2]),
        grad_wq,
        grad_wk,
        grad_wv,
        grad_bq,
        grad_bv,
        grad_wo,
        own_piece(summed[3]),
        own_piece(summed[4]),
        own_piece(summed[5]),
        grad_wu,
        grad_bu,
        grad_wd,
        own_piece(summed[6]),
    )


def solution(mesh):
    placed = (
        P(("fsdp", "tp"), None),
        P("fsdp", None),
        P(("fsdp", "tp")),
        P(("fsdp", "tp"), None),
        P(("fsdp", "tp"), None),
        P("fsdp"),
        P("fsdp"),
        P("fsdp", "tp"),
        P("fsdp", "tp"),
        P("fsdp", "tp"),
        P("tp", "fsdp"),
        P("tp", "fsdp"),
        P("tp", "fsdp"),
        P("fsdp"),
        P("fsdp"),
        P("fsdp"),
        P("fsdp", "tp"),
        P("tp", "fsdp"),
        P("tp", "fsdp"),
        P("fsdp"),
    )
    return jax.shard_map(
        local,
        mesh=mesh,
        in_specs=placed,
        out_specs=(
            P(("fsdp", "tp"), None),
            P(),
            P(("fsdp", "tp"), None),
            P("fsdp"),
            P("fsdp"),
            P("fsdp", "tp"),
            P("fsdp", "tp"),
            P("fsdp", "tp"),
            P("tp", "fsdp"),
            P("tp", "fsdp"),
            P("tp", "fsdp"),
            P("fsdp"),
            P("fsdp"),
            P("fsdp"),
            P("fsdp", "tp"),
            P("tp", "fsdp"),
            P("tp", "fsdp"),
            P("fsdp"),
        ),
        check_vma=False,
    )
```

profile of v0, /device:TPU:0, one launch (start us, length us, event | category | flops | bytes accessed | tf_op | source)
XLA Modules:
  0.0 948.7 jit_solution(11095047475518688719)
XLA Ops:
  14.4 16.0 %all-reduce.11 = (bf16[512]{0:T(512)(128)(2,1)}, bf16[512]{0:T(512)(128)(2,1)}, bf16[512]{0:T(512)(128)(2,1)}, bf16[512]{0:T(512)(128)(2,1)S(1)}, bf16[512]{0:T(512)(128)(2,1)S(1)}, /*index=5*/bf16[512]{0:T(512)(128)(2,1)}) all-reduce(bf16[512]{0:T(512)(128)(2,1)S(1)} %dynamic-update-slice.5, ...), channel_id=1, replica_groups=mesh['fsdp'=8,'tp'=4] {'fsdp'}, use_global_device_ids=true, to_apply=%add.5 | all-reduce | flops 3072 | bytes 12288
  88.5 10.3 %all-gather.7.cloned.1.call-done = bf16[3072,512]{1,0:T(8,128)(2,1)} async-done(((bf16[768,512]{1,0:T(8,128)(2,1)}), bf16[3072,512]{1,0:T(8,128)(2,1)}) %all-gather.7.cloned.1.call-update) | async-done | bytes 3145744 | tf_op jit(solution)/shard_map/all_gather | solution.py:158
  131.4 47.3 %while.54 = (s32[]{:T(128)}, bf16[3,2,512,2,64]{2,1,0,4,3:T(2,128)(2,1)}, f32[3,2,2,512]{3,2,1,0:T(2,128)}, bf16[3,2,512,2,64]{2,4,3,1,0:T(8,128)(2,1)S(1)}, s32...) while((s32[]{:T(128)}, ...), condition=%wide.region_7.8_spmd, body=%wide.region_2.7_spmd.sunk | while | flops 282656256 | bytes 17635796 | solution.py:174
  132.2 13.3 %while.57 = (s32[]{:T(128)}, bf16[2,512,2,64]{1,3,2,0:T(8,128)(2,1)S(1)}, f32[2,2,512]{2,1,0:T(2,128)S(1)}, s32[2]{0:T(128)S(1)}, s32[1024]{0:T(1024)S(1)}, /*in...) while((s32[]{:T(128)}, ...), condition=%wide.region_6.6_spmd, body=%wide.region_3.5_spmd.sunk | while | flops 282656256 | bytes 15513803 | solution.py:50
  148.0 13.3 %while.57 = (s32[]{:T(128)}, bf16[2,512,2,64]{1,3,2,0:T(8,128)(2,1)S(1)}, f32[2,2,512]{2,1,0:T(2,128)S(1)}, s32[2]{0:T(128)S(1)}, s32[1024]{0:T(1024)S(1)}, /*in...) while((s32[]{:T(128)}, ...), condition=%wide.region_6.6_spmd, body=%wide.region_3.5_spmd.sunk | while | flops 282656256 | bytes 15513803 | solution.py:50
  163.7 13.3 %while.57 = (s32[]{:T(128)}, bf16[2,512,2,64]{1,3,2,0:T(8,128)(2,1)S(1)}, f32[2,2,512]{2,1,0:T(2,128)S(1)}, s32[2]{0:T(128)S(1)}, s32[1024]{0:T(1024)S(1)}, /*in...) while((s32[]{:T(128)}, ...), condition=%wide.region_6.6_spmd, body=%wide.region_3.5_spmd.sunk | while | flops 282656256 | bytes 15513803 | solution.py:50
  184.9 58.4 %reduce-scatter.14.cloned.1.call-done = bf16[768,512]{1,0:T(8,128)(2,1)} async-done(((bf16[3072,512]{1,0:T(8,128)(2,1)}), bf16[768,512]{1,0:T(8,128)(2,1)}) %reduce-scatter.14.cloned.1.call-update) | async-done | bytes 786448 | tf_op jit(solution)/shard_map/reduce_scatter | solution.py:178
  255.8 10.8 %all_gather.70 = bf16[512,512]{1,0:T(8,128)(2,1)} all-gather(bf16[64,512]{1,0:T(8,128)(2,1)S(1)} %copy-done.38), channel_id=1, replica_groups=mesh['fsdp'=8,'tp'=4] {'fsdp'}, dimensions={0}, use_global_device_ids=true | all-gather | bytes 589824 | tf_op jit(solution)/shard_map/all_gather | solution.py:143
  276.6 33.8 %all-gather.9.cloned.1.call-done = bf16[3072,512]{1,0:T(8,128)(2,1)} async-done(((bf16[768,512]{1,0:T(8,128)(2,1)}), bf16[3072,512]{1,0:T(8,128)(2,1)}) %all-gather.9.cloned.1.call-update) | async-done | bytes 3145744 | tf_op jit(solution)/shard_map/all_gather | solution.py:186
  324.3 42.1 %psum.57 = f32[]{:T(128)} all-reduce(f32[]{:T(128)} %convert_reduce_fusion.3), channel_id=1, replica_groups=mesh['fsdp'=8,'tp'=4] {'fsdp','tp'}, use_global_device_ids=true, to_apply=%region_16.17 | all-reduce | flops 1 | bytes 8 | tf_op jit(solution)/shard_map/psum | solution.py:149
  367.1 15.9 %reduce-scatter.16.cloned.1.call-done = bf16[768,512]{1,0:T(8,128)(2,1)} async-done(((bf16[3072,512]{1,0:T(8,128)(2,1)}), bf16[768,512]{1,0:T(8,128)(2,1)}) %reduce-scatter.16.cloned.1.call-update) | async-done | bytes 786448 | tf_op jit(solution)/shard_map/reduce_scatter | solution.py:191
  388.3 63.5 %all-gather.11.cloned.1.call-done = bf16[3072,512]{1,0:T(8,128)(2,1)} async-done(((bf16[768,512]{1,0:T(8,128)(2,1)}), bf16[3072,512]{1,0:T(8,128)(2,1)}) %all-gather.11.cloned.1.call-update) | async-done | bytes 3145744 | tf_op jit(solution)/shard_map/all_gather | solution.py:205
  465.9 59.0 %reduce-scatter.18.cloned.1.call-done = bf16[768,512]{1,0:T(8,128)(2,1)} async-done(((bf16[3072,512]{1,0:T(8,128)(2,1)}), bf16[768,512]{1,0:T(8,128)(2,1)}) %reduce-scatter.18.cloned.1.call-update) | async-done | bytes 786448 | tf_op jit(solution)/shard_map/reduce_scatter | solution.py:214
  546.0 52.0 %all-gather.13.cloned.1.call-done = bf16[3072,512]{1,0:T(8,128)(2,1)} async-done(((bf16[768,512]{1,0:T(8,128)(2,1)}), bf16[3072,512]{1,0:T(8,128)(2,1)}) %all-gather.13.cloned.1.call-update) | async-done | bytes 3145744 | tf_op jit(solution)/shard_map/all_gather | solution.py:227
  607.9 69.2 %while.56 = (s32[]{:T(128)}, bf16[3,2,512,2,64]{2,4,3,1,0:T(8,128)(2,1)}, bf16[3,1024,2,64]{1,3,2,0:T(8,128)(2,1)}, bf16[3,1024,2,64]{1,3,2,0:T(8,128)(2,1)}, bf...) while((s32[]{:T(128)}, ...), condition=%wide.region_24.25_spmd, body=%wide.region_20.24_spmd.sunk | while | flops 689438208 | bytes 45550196 | solution.py:234
  610.6 17.6 %while.58 = (s32[]{:T(128)}, f32[1024,2,64]{0,2,1:T(8,128)S(1)}, f32[1024,2,64]{0,2,1:T(8,128)}, bf16[2,512,2,64]{1,3,2,0:T(8,128)(2,1)S(1)}, bf16[2,512,2,64]{1...) while((s32[]{:T(128)}, f32[1024,2,64]{0,2,1:T(8,128)S(1)}, ...), condition=%wide.region_23.23_spmd.clone, body=%wide.region_21.22_spmd.clone.sunk | while | flops 689176064 | bytes 41330992 | solution.py:82
  633.7 17.6 %while.58 = (s32[]{:T(128)}, f32[1024,2,64]{0,2,1:T(8,128)S(1)}, f32[1024,2,64]{0,2,1:T(8,128)}, bf16[2,512,2,64]{1,3,2,0:T(8,128)(2,1)S(1)}, bf16[2,512,2,64]{1...) while((s32[]{:T(128)}, f32[1024,2,64]{0,2,1:T(8,128)S(1)}, ...), condition=%wide.region_23.23_spmd.clone, body=%wide.region_21.22_spmd.clone.sunk | while | flops 689176064 | bytes 41330992 | solution.py:82
  656.8 17.6 %while.58 = (s32[]{:T(128)}, f32[1024,2,64]{0,2,1:T(8,128)S(1)}, f32[1024,2,64]{0,2,1:T(8,128)}, bf16[2,512,2,64]{1,3,2,0:T(8,128)(2,1)S(1)}, bf16[2,512,2,64]{1...) while((s32[]{:T(128)}, f32[1024,2,64]{0,2,1:T(8,128)S(1)}, ...), condition=%wide.region_23.23_spmd.clone, body=%wide.region_21.22_spmd.clone.sunk | while | flops 689176064 | bytes 41330992 | solution.py:82
  705.8 13.7 %all-reduce.10 = (bf16[2,64]{1,0:T(2,128)(2,1)S(1)}, bf16[2,64]{1,0:T(2,128)(2,1)S(1)}, bf16[8,64]{1,0:T(8,128)(2,1)S(1)}) all-reduce(bf16[2,64]{1,0:T(2,128)(2,1)S(1)} %reduce_sum.233, bf16[2,64]{1,0:T(2,128)(2,1)S(1)} %reduce_sum.234, bf16[8,64]{1,0:T(8,128)(2,1)S(1)} %convert_element_type.247), channel_id=9, replica_groups=mesh['fsdp'=8,'tp'=4] {'fsdp'}, use_global_device_ids=true, to_apply=%region_36.37.clone | all-reduce | flops 768 | bytes 3072
  722.1 33.2 %reduce-scatter.22.cloned.1.call-done = bf16[64,128]{1,0:T(8,128)(2,1)} async-done(((bf16[512,128]{1,0:T(8,128)(2,1)}), bf16[64,128]{1,0:T(8,128)(2,1)}) %reduce-scatter.22.cloned.1.call-update) | async-done | bytes 16400 | tf_op jit(solution)/shard_map/reduce_scatter | solution.py:290
  756.6 34.9 %reduce-scatter.26.cloned.1.call-done = bf16[64,128]{1,0:T(8,128)(2,1)} async-done(((bf16[512,128]{1,0:T(8,128)(2,1)}), bf16[64,128]{1,0:T(8,128)(2,1)}) %reduce-scatter.26.cloned.1.call-update) | async-done | bytes 16400 | tf_op jit(solution)/shard_map/reduce_scatter | solution.py:296
  792.9 35.3 %reduce-scatter.24.cloned.1.call-done = bf16[64,128]{1,0:T(8,128)(2,1)} async-done(((bf16[512,128]{1,0:T(8,128)(2,1)}), bf16[64,128]{1,0:T(8,128)(2,1)}) %reduce-scatter.24.cloned.1.call-update) | async-done | bytes 16400 | tf_op jit(solution)/shard_map/reduce_scatter | solution.py:293
  829.6 61.1 %reduce-scatter.20.cloned.1.call-done = bf16[768,512]{1,0:T(8,128)(2,1)} async-done(((bf16[3072,512]{1,0:T(8,128)(2,1)}), bf16[768,512]{1,0:T(8,128)(2,1)}) %reduce-scatter.20.cloned.1.call-update) | async-done | bytes 786448 | tf_op jit(solution)/shard_map/reduce_scatter | solution.py:259
  893.4 40.6 %all-reduce.9 = (f32[]{:T(128)}, f32[512]{0:T(512)S(1)}, f32[512]{0:T(512)S(1)}, f32[512]{0:T(512)S(1)}, f32[512]{0:T(512)S(1)}, /*index=5*/f32[512]{0:T(512)S(1)}, f32[512]{0:T(512)S(1)}) all-reduce(f32[]{:T(128)} %multiply_reduce_fusion.3, f32[512]{0:T(512)S(1)} %get-tuple-element.340, ...), channel_id=1, replica_groups=mesh['fsdp'=8,'tp'=4] {'fsdp','tp'}, use_global_device_ids=true, to_apply=%region_14.15 | all-reduce | flops 3073 | bytes 24584 | tf_op jit(solution)/shard_map/psum | solution.py:270
  (474 shorter events, 339.5 us)
Async XLA Ops:
  7.2 91.5 %all-gather.7.cloned.1.call-start = ((), (), s32[]{:S(2)}) async-start(), calls=%async_computation.10 | async-start | bytes 3932160 | tf_op jit(solution)/shard_map/all_gather | solution.py:158
  35.7 207.5 %reduce-scatter.14.cloned.1.call-start = ((), (), s32[]{:S(2)}) async-start(), calls=%async_computation.11 | async-start | bytes 3932160 | tf_op jit(solution)/shard_map/reduce_scatter | solution.py:178
  184.2 126.2 %all-gather.9.cloned.1.call-start = ((), (), s32[]{:S(2)}) async-start(), calls=%async_computation.12 | async-start | bytes 3932160 | tf_op jit(solution)/shard_map/all_gather | solution.py:186
  246.7 136.3 %reduce-scatter.16.cloned.1.call-start = ((), (), s32[]{:S(2)}) async-start(), calls=%async_computation.13 | async-start | bytes 3932160 | tf_op jit(solution)/shard_map/reduce_scatter | solution.py:191
  323.0 128.8 %all-gather.11.cloned.1.call-start = ((), (), s32[]{:S(2)}) async-start(), calls=%async_computation.14 | async-start | bytes 3932160 | tf_op jit(solution)/shard_map/all_gather | solution.py:205
  388.1 136.9 %reduce-scatter.18.cloned.1.call-start = ((), (), s32[]{:S(2)}) async-start(), calls=%async_computation.15 | async-start | bytes 3932160 | tf_op jit(solution)/shard_map/reduce_scatter | solution.py:214
  465.9 132.1 %all-gather.13.cloned.1.call-start = ((), (), s32[]{:S(2)}) async-start(), calls=%async_computation.16 | async-start | bytes 3932160 | tf_op jit(solution)/shard_map/all_gather | solution.py:227
  534.3 167.4 %reduce-scatter.32.cloned.1.call-start = ((), (), s32[]{:S(2)}) async-start(), calls=%async_computation.23 | async-start | bytes 589824 | tf_op jit(solution)/shard_map/reduce_scatter | solution.py:314
  539.9 163.3 %reduce-scatter.30.cloned.1.call-start = ((), (), s32[]{:S(2)}) async-start(), calls=%async_computation.22 | async-start | bytes 589824 | tf_op jit(solution)/shard_map/reduce_scatter | solution.py:308
  546.0 174.8 %reduce-scatter.28.cloned.1.call-start = ((), (), s32[]{:S(2)}) async-start(), calls=%async_computation.21 | async-start | bytes 147456 | tf_op jit(solution)/shard_map/reduce_scatter | solution.py:305
  686.5 68.8 %reduce-scatter.22.cloned.1.call-start = ((), (), s32[]{:S(2)}) async-start(), calls=%async_computation.18 | async-start | bytes 147456 | tf_op jit(solution)/shard_map/reduce_scatter | solution.py:290
  689.6 101.9 %reduce-scatter.26.cloned.1.call-start = ((), (), s32[]{:S(2)}) async-start(), calls=%async_computation.20 | async-start | bytes 147456 | tf_op jit(solution)/shard_map/reduce_scatter | solution.py:296
  692.5 135.7 %reduce-scatter.24.cloned.1.call-start = ((), (), s32[]{:S(2)}) async-start(), calls=%async_computation.19 | async-start | bytes 147456 | tf_op jit(solution)/shard_map/reduce_scatter | solution.py:293
  695.5 195.2 %reduce-scatter.20.cloned.1.call-start = ((), (), s32[]{:S(2)}) async-start(), calls=%async_computation.17 | async-start | bytes 3932160 | tf_op jit(solution)/shard_map/reduce_scatter | solution.py:259
  700.7 190.0 %copy-start.2 = (bf16[768,512]{1,0:T(8,128)(2,1)S(1)}, bf16[768,512]{1,0:T(8,128)(2,1)}, u32[]{:S(2)}) copy-start(bf16[768,512]{1,0:T(8,128)(2,1)} %param.28) | copy-start | bytes 2359300
  700.7 189.9 %copy-start.36 = (f32[768]{0:T(1024)S(1)}, f32[768]{0:T(1024)}, u32[]{:S(2)}) copy-start(f32[768]{0:T(1024)} %copy-done.35) | copy-start | bytes 9220
  700.7 189.9 %copy-start.43 = (f32[512]{0:T(512)S(1)}, f32[512]{0:T(512)}, u32[]{:S(2)}) copy-start(f32[512]{0:T(512)} %copy-done.42) | copy-start | bytes 6148
  700.8 191.7 %copy-start.45 = (f32[768]{0:T(1024)S(1)}, f32[768]{0:T(1024)}, u32[]{:S(2)}) copy-start(f32[768]{0:T(1024)} %copy-done.44) | copy-start | bytes 9220
  700.8 191.7 %copy-start.41 = (f32[768]{0:T(1024)S(1)}, f32[768]{0:T(1024)}, u32[]{:S(2)}) copy-start(f32[768]{0:T(1024)} %copy-done.40) | copy-start | bytes 9220
  705.5 187.9 %copy-start.53 = (f32[512]{0:T(512)S(1)}, f32[512]{0:T(512)}, u32[]{:S(2)}) copy-start(f32[512]{0:T(512)} %get-tuple-element.437) | copy-start | bytes 6148
  705.5 187.9 %copy-start.54 = (f32[512]{0:T(512)S(1)}, f32[512]{0:T(512)}, u32[]{:S(2)}) copy-start(f32[512]{0:T(512)} %get-tuple-element.338) | copy-start | bytes 6148
  705.5 187.9 %copy-start.55 = (f32[512]{0:T(512)S(1)}, f32[512]{0:T(512)}, u32[]{:S(2)}) copy-start(f32[512]{0:T(512)} %get-tuple-element.439) | copy-start | bytes 6148
  705.5 187.9 %copy-start.56 = (f32[512]{0:T(512)S(1)}, f32[512]{0:T(512)}, u32[]{:S(2)}) copy-start(f32[512]{0:T(512)} %get-tuple-element.343) | copy-start | bytes 6148
  705.5 233.4 %copy-start.11 = (f32[768,512]{1,0:T(8,128)S(1)}, f32[768,512]{1,0:T(8,128)}, u32[]{:S(2)}) copy-start(f32[768,512]{1,0:T(8,128)} %copy-done.10) | copy-start | bytes 4718596
  (67 other events, 708.7 us)
Sparse Core Ops, SparseCore 0:
  35.8 62.8 all-gather.6
  184.3 58.8 reduce-scatter.13
  246.8 63.5 all-gather.8
  323.2 59.8 reduce-scatter.15
  388.2 63.5 all-gather.10
  466.0 58.8 reduce-scatter.17
  534.4 63.5 all-gather.12
  601.1 32.8 reduce-scatter.31
  637.4 34.1 reduce-scatter.29
  686.6 31.9 reduce-scatter.27
  721.9 33.3 reduce-scatter.21
  758.2 33.3 reduce-scatter.25
  794.8 33.3 reduce-scatter.23
  830.4 60.2 reduce-scatter.19
where the time goes:
time: 957 us; the launch traced here: 949 us
  waiting for transfers between devices  458 us (48%)
  blocking collectives  194 us (20%)
  matrix products  117 us (12%)
  local copies, waits for them, and re-layouts  86.9 us (9%)
  other arithmetic  63 us (7%)
  between operations  19.7 us (2%)
    all_gather x1, waiting for transfers between devices, local(): grad_rows = lax.all_gather(grad_out_low, 'tp', axis=0, tiled=True)  63.5 us
    reduce_scatter x1, waiting for transfers between devices, local(): lax.psum_scatter(jnp.einsum('nc,dc->nd', stacked_grads, stacked_weights,...  61.1 us
    reduce_scatter x1, waiting for transfers between devices, local(): lax.psum_scatter(jnp.einsum('nf,df->nd', grad_pre, upper_w, preferred_ele...  59 us
    reduce_scatter x1, waiting for transfers between devices, local(): lax.psum_scatter(jnp.dot(attended, out_w, preferred_element_type=jnp.floa...  58.4 us
    all_gather x1, waiting for transfers between devices, local(): grad_attn_rows = lax.all_gather(grad_attn_low, 'tp', axis=0, tiled=True)  52 us
    psum x1, blocking collectives, local(): valid_total = lax.psum(jnp.sum(mask_float), ('fsdp', 'tp'))  42.1 us
    psum x1, blocking collectives, local(): lax.psum((square_part, grad_gain_first, grad_bias_first, grad_out_bias, g...  40.6 us
    reduce_scatter x1, waiting for transfers between devices, local(): lax.psum_scatter(grad_key_w.astype(jnp.bfloat16), 'fsdp', scatter_dimensi...  35.3 us
  transfers between devices with their start and end apart: 14, of which 11 were waited for; matrix products, arithmetic and copies ran while one was open for 13% of the time, Pallas kernels for 0%

commit v1 on v0

--- a/solution.py
+++ b/solution.py
@@ -183,7 +183,10 @@
     ).astype(jnp.float32)
     hidden_one = input_float + attention + out_b.astype(jnp.float32)
     normed_two = layer_norm(hidden_one, gain_second, bias_second).astype(jnp.bfloat16)
-    rows_two = lax.all_gather(normed_two, "tp", axis=0, tiled=True)
+    size = lax.axis_size("tp")
+    blocks = jnp.stack([normed_two for _ in range(size)])
+    blocks = lax.all_to_all(blocks, "tp", split_axis=0, concat_axis=0)
+    rows_two = jnp.concatenate(blocks, axis=0)
     pre_act = jnp.dot(rows_two, upper_w, preferred_element_type=jnp.float32) + upper_b.reshape(
         -1
     ).astype(jnp.float32)

time: 957 us -> 967 us (1.010)
    all_to_all x0 -> x1, waiting for transfers between devices: none -> 41 us  [local(): blocks = lax.all_to_all(blocks, 'tp', split_axis=0, concat_axis=0)]
    all_gather x1 -> x0, waiting for transfers between devices: 33.8 us -> none  [local(): rows_two = lax.all_gather(normed_two, 'tp', axis=0, tiled=True)]
where the time goes in v1:
time: 967 us; the launch traced here: 959 us
  waiting for transfers between devices  465 us (48%)
  blocking collectives  195 us (20%)
  matrix products  111 us (11%)
  local copies, waits for them, and re-layouts  91.8 us (9%)
  other arithmetic  62.1 us (6%)
  between operations  19.6 us (2%)
    all_gather x1, waiting for transfers between devices, local(): grad_rows = lax.all_gather(grad_out_low, 'tp', axis=0, tiled=True)  63.5 us
    reduce_scatter x1, waiting for transfers between devices, local(): lax.psum_scatter(jnp.einsum('nc,dc->nd', stacked_grads, stacked_weights,...  61.3 us
    reduce_scatter x1, waiting for transfers between devices, local(): lax.psum_scatter(jnp.einsum('nf,df->nd', grad_pre, upper_w, preferred_ele...  59 us
    reduce_scatter x1, waiting for transfers between devices, local(): lax.psum_scatter(jnp.dot(attended, out_w, preferred_element_type=jnp.floa...  58.4 us
    all_gather x1, waiting for transfers between devices, local(): grad_attn_rows = lax.all_gather(grad_attn_low, 'tp', axis=0, tiled=True)  52 us
    psum x1, blocking collectives, local(): valid_total = lax.psum(jnp.sum(mask_float), ('fsdp', 'tp'))  42.5 us
    all_to_all x1, waiting for transfers between devices, local(): blocks = lax.all_to_all(blocks, 'tp', split_axis=0, concat_axis=0)  41 us
    psum x1, blocking collectives, local(): lax.psum((square_part, grad_gain_first, grad_bias_first, grad_out_bias, g...  40.7 us
  transfers between devices with their start and end apart: 14, of which 11 were waited for; matrix products, arithmetic and copies ran while one was open for 13% of the time, Pallas kernels for 0%

profile of v1, /device:TPU:0, one launch (start us, length us, event | category | flops | bytes accessed | tf_op | source)
XLA Modules:
  0.0 959.0 jit_solution(1761160920472941449)
XLA Ops:
  14.4 16.0 %all-reduce.11 = (bf16[512]{0:T(512)(128)(2,1)}, bf16[512]{0:T(512)(128)(2,1)}, bf16[512]{0:T(512)(128)(2,1)}, bf16[512]{0:T(512)(128)(2,1)S(1)}, bf16[512]{0:T(512)(128)(2,1)S(1)}, /*index=5*/bf16[512]{0:T(512)(128)(2,1)}) all-reduce(bf16[512]{0:T(512)(128)(2,1)S(1)} %dynamic-update-slice.5, ...), channel_id=1, replica_groups=mesh['fsdp'=8,'tp'=4] {'fsdp'}, use_global_device_ids=true, to_apply=%add.5 | all-reduce | flops 3072 | bytes 12288
  88.5 10.3 %all-gather.6.cloned.1.call-done = bf16[3072,512]{1,0:T(8,128)(2,1)} async-done(((bf16[768,512]{1,0:T(8,128)(2,1)}), bf16[3072,512]{1,0:T(8,128)(2,1)}) %all-gather.6.cloned.1.call-update) | async-done | bytes 3145744 | tf_op jit(solution)/shard_map/all_gather | solution.py:158
  131.4 41.6 %while.54 = (s32[]{:T(128)}, bf16[3,2,512,2,64]{2,1,0,4,3:T(2,128)(2,1)}, f32[3,2,2,512]{3,2,1,0:T(2,128)}, bf16[3,2,512,2,64]{2,4,3,1,0:T(8,128)(2,1)S(1)}, s32...) while((s32[]{:T(128)}, ...), condition=%wide.region_7.8_spmd, body=%wide.region_2.7_spmd.sunk | while | flops 282656256 | bytes 17635796 | solution.py:174
  132.3 11.4 %while.57 = (s32[]{:T(128)}, bf16[2,512,2,64]{1,3,2,0:T(8,128)(2,1)S(1)}, f32[2,2,512]{2,1,0:T(2,128)S(1)}, s32[2]{0:T(128)S(1)}, s32[1024]{0:T(1024)S(1)}, /*in...) while((s32[]{:T(128)}, ...), condition=%wide.region_6.6_spmd, body=%wide.region_3.5_spmd.sunk | while | flops 282656256 | bytes 15513803 | solution.py:50
  146.1 11.5 %while.57 = (s32[]{:T(128)}, bf16[2,512,2,64]{1,3,2,0:T(8,128)(2,1)S(1)}, f32[2,2,512]{2,1,0:T(2,128)S(1)}, s32[2]{0:T(128)S(1)}, s32[1024]{0:T(1024)S(1)}, /*in...) while((s32[]{:T(128)}, ...), condition=%wide.region_6.6_spmd, body=%wide.region_3.5_spmd.sunk | while | flops 282656256 | bytes 15513803 | solution.py:50
  160.0 11.4 %while.57 = (s32[]{:T(128)}, bf16[2,512,2,64]{1,3,2,0:T(8,128)(2,1)S(1)}, f32[2,2,512]{2,1,0:T(2,128)S(1)}, s32[2]{0:T(128)S(1)}, s32[1024]{0:T(1024)S(1)}, /*in...) while((s32[]{:T(128)}, ...), condition=%wide.region_6.6_spmd, body=%wide.region_3.5_spmd.sunk | while | flops 282656256 | bytes 15513803 | solution.py:50
  179.7 58.4 %reduce-scatter.14.cloned.1.call-done = bf16[768,512]{1,0:T(8,128)(2,1)} async-done(((bf16[3072,512]{1,0:T(8,128)(2,1)}), bf16[768,512]{1,0:T(8,128)(2,1)}) %reduce-scatter.14.cloned.1.call-update) | async-done | bytes 786448 | tf_op jit(solution)/shard_map/reduce_scatter | solution.py:178
  256.4 10.8 %all_gather.66 = bf16[512,512]{1,0:T(8,128)(2,1)} all-gather(bf16[64,512]{1,0:T(8,128)(2,1)S(1)} %copy-done.37), channel_id=1, replica_groups=mesh['fsdp'=8,'tp'=4] {'fsdp'}, dimensions={0}, use_global_device_ids=true | all-gather | bytes 589824 | tf_op jit(solution)/shard_map/all_gather | solution.py:143
  277.1 41.0 %all-to-all-done = bf16[4,768,512]{2,1,0:T(8,128)(2,1)} async-done(((bf16[4,768,512]{2,1,0:T(8,128)(2,1)}), bf16[4,768,512]{2,1,0:T(8,128)(2,1)}, u32[]{:S(2)}, u32[]{:S(2)}) %all-to-all-start) | async-done | bytes 3145760 | tf_op jit(solution)/shard_map/all_to_all | solution.py:188
  332.0 42.5 %psum.57 = f32[]{:T(128)} all-reduce(f32[]{:T(128)} %convert_reduce_fusion.3), channel_id=1, replica_groups=mesh['fsdp'=8,'tp'=4] {'fsdp','tp'}, use_global_device_ids=true, to_apply=%region_16.17 | all-reduce | flops 1 | bytes 8 | tf_op jit(solution)/shard_map/psum | solution.py:149
  375.2 16.0 %reduce-scatter.16.cloned.1.call-done = bf16[768,512]{1,0:T(8,128)(2,1)} async-done(((bf16[3072,512]{1,0:T(8,128)(2,1)}), bf16[768,512]{1,0:T(8,128)(2,1)}) %reduce-scatter.16.cloned.1.call-update) | async-done | bytes 786448 | tf_op jit(solution)/shard_map/reduce_scatter | solution.py:194
  396.4 63.5 %all-gather.8.cloned.1.call-done = bf16[3072,512]{1,0:T(8,128)(2,1)} async-done(((bf16[768,512]{1,0:T(8,128)(2,1)}), bf16[3072,512]{1,0:T(8,128)(2,1)}) %all-gather.8.cloned.1.call-update) | async-done | bytes 3145744 | tf_op jit(solution)/shard_map/all_gather | solution.py:208
  474.0 59.0 %reduce-scatter.18.cloned.1.call-done = bf16[768,512]{1,0:T(8,128)(2,1)} async-done(((bf16[3072,512]{1,0:T(8,128)(2,1)}), bf16[768,512]{1,0:T(8,128)(2,1)}) %reduce-scatter.18.cloned.1.call-update) | async-done | bytes 786448 | tf_op jit(solution)/shard_map/reduce_scatter | solution.py:217
  554.1 52.0 %all-gather.10.cloned.1.call-done = bf16[3072,512]{1,0:T(8,128)(2,1)} async-done(((bf16[768,512]{1,0:T(8,128)(2,1)}), bf16[3072,512]{1,0:T(8,128)(2,1)}) %all-gather.10.cloned.1.call-update) | async-done | bytes 3145744 | tf_op jit(solution)/shard_map/all_gather | solution.py:230
  615.9 71.3 %while.56 = (s32[]{:T(128)}, bf16[3,2,512,2,64]{2,4,3,1,0:T(8,128)(2,1)}, bf16[3,1024,2,64]{1,3,2,0:T(8,128)(2,1)}, bf16[3,1024,2,64]{1,3,2,0:T(8,128)(2,1)}, bf...) while((s32[]{:T(128)}, ...), condition=%wide.region_24.25_spmd, body=%wide.region_20.24_spmd.sunk | while | flops 689438208 | bytes 45550196 | solution.py:237
  619.4 17.6 %while.58 = (s32[]{:T(128)}, f32[1024,2,64]{0,2,1:T(8,128)S(1)}, f32[1024,2,64]{0,2,1:T(8,128)}, bf16[2,512,2,64]{1,3,2,0:T(8,128)(2,1)S(1)}, bf16[2,512,2,64]{1...) while((s32[]{:T(128)}, f32[1024,2,64]{0,2,1:T(8,128)S(1)}, ...), condition=%wide.region_23.23_spmd.clone, body=%wide.region_21.22_spmd.clone.sunk | while | flops 689176064 | bytes 41330992 | solution.py:82
  643.1 17.6 %while.58 = (s32[]{:T(128)}, f32[1024,2,64]{0,2,1:T(8,128)S(1)}, f32[1024,2,64]{0,2,1:T(8,128)}, bf16[2,512,2,64]{1,3,2,0:T(8,128)(2,1)S(1)}, bf16[2,512,2,64]{1...) while((s32[]{:T(128)}, f32[1024,2,64]{0,2,1:T(8,128)S(1)}, ...), condition=%wide.region_23.23_spmd.clone, body=%wide.region_21.22_spmd.clone.sunk | while | flops 689176064 | bytes 41330992 | solution.py:82
  666.9 17.6 %while.58 = (s32[]{:T(128)}, f32[1024,2,64]{0,2,1:T(8,128)S(1)}, f32[1024,2,64]{0,2,1:T(8,128)}, bf16[2,512,2,64]{1,3,2,0:T(8,128)(2,1)S(1)}, bf16[2,512,2,64]{1...) while((s32[]{:T(128)}, f32[1024,2,64]{0,2,1:T(8,128)S(1)}, ...), condition=%wide.region_23.23_spmd.clone, body=%wide.region_21.22_spmd.clone.sunk | while | flops 689176064 | bytes 41330992 | solution.py:82
  716.0 13.7 %all-reduce.10 = (bf16[2,64]{1,0:T(2,128)(2,1)S(1)}, bf16[2,64]{1,0:T(2,128)(2,1)S(1)}, bf16[8,64]{1,0:T(8,128)(2,1)S(1)}) all-reduce(bf16[2,64]{1,0:T(2,128)(2,1)S(1)} %reduce_sum.233, bf16[2,64]{1,0:T(2,128)(2,1)S(1)} %reduce_sum.234, bf16[8,64]{1,0:T(8,128)(2,1)S(1)} %convert_element_type.247), channel_id=9, replica_groups=mesh['fsdp'=8,'tp'=4] {'fsdp'}, use_global_device_ids=true, to_apply=%region_36.37.clone | all-reduce | flops 768 | bytes 3072
  732.3 33.0 %reduce-scatter.22.cloned.1.call-done = bf16[64,128]{1,0:T(8,128)(2,1)} async-done(((bf16[512,128]{1,0:T(8,128)(2,1)}), bf16[64,128]{1,0:T(8,128)(2,1)}) %reduce-scatter.22.cloned.1.call-update) | async-done | bytes 16400 | tf_op jit(solution)/shard_map/reduce_scatter | solution.py:293
  766.7 35.1 %reduce-scatter.26.cloned.1.call-done = bf16[64,128]{1,0:T(8,128)(2,1)} async-done(((bf16[512,128]{1,0:T(8,128)(2,1)}), bf16[64,128]{1,0:T(8,128)(2,1)}) %reduce-scatter.26.cloned.1.call-update) | async-done | bytes 16400 | tf_op jit(solution)/shard_map/reduce_scatter | solution.py:299
  803.1 35.2 %reduce-scatter.24.cloned.1.call-done = bf16[64,128]{1,0:T(8,128)(2,1)} async-done(((bf16[512,128]{1,0:T(8,128)(2,1)}), bf16[64,128]{1,0:T(8,128)(2,1)}) %reduce-scatter.24.cloned.1.call-update) | async-done | bytes 16400 | tf_op jit(solution)/shard_map/reduce_scatter | solution.py:296
  839.6 61.3 %reduce-scatter.20.cloned.1.call-done = bf16[768,512]{1,0:T(8,128)(2,1)} async-done(((bf16[3072,512]{1,0:T(8,128)(2,1)}), bf16[768,512]{1,0:T(8,128)(2,1)}) %reduce-scatter.20.cloned.1.call-update) | async-done | bytes 786448 | tf_op jit(solution)/shard_map/reduce_scatter | solution.py:262
  903.7 40.7 %all-reduce.9 = (f32[]{:T(128)}, f32[512]{0:T(512)S(1)}, f32[512]{0:T(512)S(1)}, f32[512]{0:T(512)S(1)}, f32[512]{0:T(512)S(1)}, /*index=5*/f32[512]{0:T(512)S(1)}, f32[512]{0:T(512)S(1)}) all-reduce(f32[]{:T(128)} %multiply_reduce_fusion.3, f32[512]{0:T(512)S(1)} %get-tuple-element.340, ...), channel_id=1, replica_groups=mesh['fsdp'=8,'tp'=4] {'fsdp','tp'}, use_global_device_ids=true, to_apply=%region_14.15 | all-reduce | flops 3073 | bytes 24584 | tf_op jit(solution)/shard_map/psum | solution.py:273
  (472 shorter events, 342.1 us)
Async XLA Ops:
  7.2 91.5 %all-gather.6.cloned.1.call-start = ((), (), s32[]{:S(2)}) async-start(), calls=%async_computation.11 | async-start | bytes 3932160 | tf_op jit(solution)/shard_map/all_gather | solution.py:158
  35.7 202.3 %reduce-scatter.14.cloned.1.call-start = ((), (), s32[]{:S(2)}) async-start(), calls=%async_computation.12 | async-start | bytes 3932160 | tf_op jit(solution)/shard_map/reduce_scatter | solution.py:178
  242.5 75.6 %all-to-all-start = ((bf16[4,768,512]{2,1,0:T(8,128)(2,1)}), bf16[4,768,512]{2,1,0:T(8,128)(2,1)}, u32[]{:S(2)}, u32[]{:S(2)}) async-start(bf16[4,768,512]{2,1,0:T(8,128)(2,1)} %stack.2), calls=%async_computation.1 | async-start | bytes 6291456 | tf_op jit(solution)/shard_map/all_to_all | solution.py:188
  247.3 143.9 %reduce-scatter.16.cloned.1.call-start = ((), (), s32[]{:S(2)}) async-start(), calls=%async_computation.13 | async-start | bytes 3932160 | tf_op jit(solution)/shard_map/reduce_scatter | solution.py:194
  330.8 129.2 %all-gather.8.cloned.1.call-start = ((), (), s32[]{:S(2)}) async-start(), calls=%async_computation.14 | async-start | bytes 3932160 | tf_op jit(solution)/shard_map/all_gather | solution.py:208
  396.2 136.8 %reduce-scatter.18.cloned.1.call-start = ((), (), s32[]{:S(2)}) async-start(), calls=%async_computation.15 | async-start | bytes 3932160 | tf_op jit(solution)/shard_map/reduce_scatter | solution.py:217
  474.0 132.1 %all-gather.10.cloned.1.call-start = ((), (), s32[]{:S(2)}) async-start(), calls=%async_computation.16 | async-start | bytes 3932160 | tf_op jit(solution)/shard_map/all_gather | solution.py:230
  542.4 169.5 %reduce-scatter.32.cloned.1.call-start = ((), (), s32[]{:S(2)}) async-start(), calls=%async_computation.23 | async-start | bytes 589824 | tf_op jit(solution)/shard_map/reduce_scatter | solution.py:317
  548.0 165.4 %reduce-scatter.30.cloned.1.call-start = ((), (), s32[]{:S(2)}) async-start(), calls=%async_computation.22 | async-start | bytes 589824 | tf_op jit(solution)/shard_map/reduce_scatter | solution.py:311
  554.0 176.9 %reduce-scatter.28.cloned.1.call-start = ((), (), s32[]{:S(2)}) async-start(), calls=%async_computation.21 | async-start | bytes 147456 | tf_op jit(solution)/shard_map/reduce_scatter | solution.py:308
  696.6 68.7 %reduce-scatter.22.cloned.1.call-start = ((), (), s32[]{:S(2)}) async-start(), calls=%async_computation.18 | async-start | bytes 147456 | tf_op jit(solution)/shard_map/reduce_scatter | solution.py:293
  699.8 102.0 %reduce-scatter.26.cloned.1.call-start = ((), (), s32[]{:S(2)}) async-start(), calls=%async_computation.20 | async-start | bytes 147456 | tf_op jit(solution)/shard_map/reduce_scatter | solution.py:299
  702.7 135.6 %reduce-scatter.24.cloned.1.call-start = ((), (), s32[]{:S(2)}) async-start(), calls=%async_computation.19 | async-start | bytes 147456 | tf_op jit(solution)/shard_map/reduce_scatter | solution.py:296
  705.7 195.2 %reduce-scatter.20.cloned.1.call-start = ((), (), s32[]{:S(2)}) async-start(), calls=%async_computation.17 | async-start | bytes 3932160 | tf_op jit(solution)/shard_map/reduce_scatter | solution.py:262
  710.9 190.0 %copy-start.2 = (bf16[768,512]{1,0:T(8,128)(2,1)S(1)}, bf16[768,512]{1,0:T(8,128)(2,1)}, u32[]{:S(2)}) copy-start(bf16[768,512]{1,0:T(8,128)(2,1)} %param.28) | copy-start | bytes 2359300
  710.9 190.0 %copy-start.36 = (f32[768]{0:T(1024)S(1)}, f32[768]{0:T(1024)}, u32[]{:S(2)}) copy-start(f32[768]{0:T(1024)} %copy-done.35) | copy-start | bytes 9220
  710.9 190.0 %copy-start.42 = (f32[512]{0:T(512)S(1)}, f32[512]{0:T(512)}, u32[]{:S(2)}) copy-start(f32[512]{0:T(512)} %copy-done.41) | copy-start | bytes 6148
  711.0 191.7 %copy-start.44 = (f32[768]{0:T(1024)S(1)}, f32[768]{0:T(1024)}, u32[]{:S(2)}) copy-start(f32[768]{0:T(1024)} %copy-done.43) | copy-start | bytes 9220
  711.0 191.7 %copy-start.40 = (f32[768]{0:T(1024)S(1)}, f32[768]{0:T(1024)}, u32[]{:S(2)}) copy-start(f32[768]{0:T(1024)} %copy-done.39) | copy-start | bytes 9220
  715.7 187.9 %copy-start.52 = (f32[512]{0:T(512)S(1)}, f32[512]{0:T(512)}, u32[]{:S(2)}) copy-start(f32[512]{0:T(512)} %get-tuple-element.437) | copy-start | bytes 6148
  715.7 187.9 %copy-start.53 = (f32[512]{0:T(512)S(1)}, f32[512]{0:T(512)}, u32[]{:S(2)}) copy-start(f32[512]{0:T(512)} %get-tuple-element.338) | copy-start | bytes 6148
  715.7 187.9 %copy-start.54 = (f32[512]{0:T(512)S(1)}, f32[512]{0:T(512)}, u32[]{:S(2)}) copy-start(f32[512]{0:T(512)} %get-tuple-element.439) | copy-start | bytes 6148
  715.7 187.9 %copy-start.55 = (f32[512]{0:T(512)S(1)}, f32[512]{0:T(512)}, u32[]{:S(2)}) copy-start(f32[512]{0:T(512)} %get-tuple-element.343) | copy-start | bytes 6148
  715.8 233.4 %copy-start.11 = (f32[768,512]{1,0:T(8,128)S(1)}, f32[768,512]{1,0:T(8,128)}, u32[]{:S(2)}) copy-start(f32[768,512]{1,0:T(8,128)} %copy-done.10) | copy-start | bytes 4718596
  (66 other events, 706.0 us)
Sparse Core Ops, SparseCore 0:
  35.8 62.8 all-gather.5
  179.1 58.8 reduce-scatter.13
  330.9 60.2 reduce-scatter.15
  396.3 63.5 all-gather.7
  474.1 58.8 reduce-scatter.17
  542.5 63.5 all-gather.9
  609.1 32.8 reduce-scatter.31
  645.4 34.0 reduce-scatter.29
  696.8 32.0 reduce-scatter.27
  732.0 33.3 reduce-scatter.21
  768.4 33.3 reduce-scatter.25
  804.9 33.3 reduce-scatter.23
  840.6 60.2 reduce-scatter.19
